TPU v7x, 32 devices: a whole 2x2x4 slice. The times are simulated.
32 devices in a mesh: users: 8 (over z, y), items: 4 (over x, core).
Axes of the slice: x: 2, y: 2, z: 4, core: 2. Of those that a mesh axis runs over, the one named last changes fastest.
Arguments:
- tile_rows: int32 [8, 4, 512], P('users', 'items'), may hold values from 0 to 63, as said below
- tile_cols: int32 [8, 4, 512], P('users', 'items'), may hold values from 0 to 63, as said below
- tile_count: int32 [8, 4], P('users', 'items'), may hold values from 64 to 512, as said below
- tile_vals: bfloat16 [8, 4, 512, 128, 128], P('users', 'items'), may hold values from -6 to 6
- user_degree: int32 [65536], P(('users', 'items')), may hold values from 16 to 575
- item_degree: int32 [32768], P(('items', 'users')), may hold values from 16 to 575
- start_items: bfloat16 [64, 32768], P(None, ('items', 'users')), may hold values from -6 to 6
Outputs:
- user_panel: float32 [64, 65536], P(None, ('users', 'items'))
- item_panel: float32 [64, 32768], P(None, ('items', 'users'))
Inputs may be any that keep to these rules, and one draw needn't show every extreme that they name: Within one user block and item block, the pairs (tile_rows, tile_cols) of all 512 slots are distinct. `tile_cols`: paired with tile_rows slot by slot. Only the first tile_count slots of a block are live; some block is full in every draw.
All inputs are finite; a program needn't handle non-finite values.
Results may differ from a plain program's by a relative error of at most 0.0003.
Values sent between devices are 32-bit elements; how exact they have to be, the bound alone decides.
No kernel may reach another device: no remote copies, remote signals or barrier semaphores. Data moves between devices by JAX's collectives and lax.ppermute only.
A program may use at most 128 MiB of HBM per device.

v0:
```python
import jax
import jax.numpy as jnp
from jax import lax
from jax.sharding import PartitionSpec as P

K = 64
TILE = 128
ITERS = 2
UT = 64
IT = 64


def local_gram(raw):
    return jnp.einsum(
        "kr,jr->kj", raw, raw, precision=lax.Precision.HIGHEST, preferred_element_type=jnp.float32
    )


def solve_panel(gram, raw):
    lower = jnp.linalg.cholesky(gram)
    return lax.linalg.triangular_solve(lower, raw, left_side=True, lower=True)


def user_partial(full_items, rows, cols, values, live_weight):
    picked = jnp.take(full_items.reshape(K, IT, TILE), cols, axis=1)
    product = jnp.einsum(
        "ktc,trc->ktr",
        picked,
        values,
        precision=lax.Precision.HIGHEST,
        preferred_element_type=jnp.float32,
    )
    product = product * live_weight[None, :, None]
    summed = jnp.zeros((K, UT, TILE), jnp.float32).at[:, rows, :].add(product)
    return summed.reshape(K, UT * TILE)


def item_partial(full_users, rows, cols, values, live_weight):
    picked = jnp.take(full_users.reshape(K, UT, TILE), rows, axis=1)
    product = jnp.einsum(
        "ktr,trc->ktc",
        picked,
        values,
        precision=lax.Precision.HIGHEST,
        preferred_element_type=jnp.float32,
    )
    product = product * live_weight[None, :, None]
    summed = jnp.zeros((K, IT, TILE), jnp.float32).at[:, cols, :].add(product)
    return summed.reshape(K, IT * TILE)


def gather_items(sent):
    return lax.all_gather(sent, "users", axis=1, tiled=True)


def body(tile_rows, tile_cols, tile_count, tile_vals, user_degree, item_degree, start_items):
    rows = tile_rows[0, 0]
    cols = tile_cols[0, 0]
    values = tile_vals[0, 0].astype(jnp.float32)
    slots = values.shape[0]
    live_weight = (jnp.arange(slots, dtype=jnp.int32) < tile_count[0, 0]).astype(jnp.float32)
    user_scale = lax.rsqrt(user_degree.astype(jnp.float32))
    item_scale = lax.rsqrt(item_degree.astype(jnp.float32))
    user_groups = lax.axis_size("users")
    item_groups = lax.axis_size("items")
    user_total = UT * TILE * user_groups
    item_total = IT * TILE * item_groups
    user_width = UT * TILE // item_groups
    item_width = IT * TILE // user_groups
    item_scale_block = lax.all_gather(item_scale, "users", axis=0, tiled=True)
    panel = start_items.astype(jnp.float32)
    user_panel = jnp.zeros((K, user_width), jnp.float32)
    for step in range(ITERS):
        if step == 0:
            full_items = gather_items(item_scale[None, :] * panel)
        else:
            full_items = item_scale_block[None, :] * panel
        partial_users = user_partial(full_items, rows, cols, values, live_weight)
        user_raw = user_scale[None, :] * lax.psum_scatter(
            partial_users, "items", scatter_dimension=1, tiled=True
        )
        user_gram = lax.psum(local_gram(user_raw), ("users", "items"))
        user_panel = solve_panel(user_gram / user_total, user_raw)
        full_users = lax.all_gather(user_scale[None, :] * user_panel, "items", axis=1, tiled=True)
        partial_items = item_partial(full_users, rows, cols, values, live_weight)
        item_raw = item_scale_block[None, :] * lax.psum(partial_items, "users")
        item_gram = lax.psum(local_gram(item_raw), "items")
        panel = solve_panel(item_gram / item_total, item_raw)
    item_out = lax.dynamic_slice_in_dim(panel, lax.axis_index("users") * item_width, item_width, 1)
    return (user_panel, item_out)


def solution(mesh):
    in_specs = (
        P("users", "items", None),
        P("users", "items", None),
        P("users", "items"),
        P("users", "items", None, None, None),
        P(("users", "items")),
        P(("items", "users")),
        P(None, ("items", "users")),
    )
    out_specs = (P(None, ("users", "items")), P(None, ("items", "users")))
    return jax.shard_map(body, mesh=mesh, in_specs=in_specs, out_specs=out_specs, check_vma=False)
```

profile of v0, /device:TPU:0, one launch (start us, length us, event | category | flops | bytes accessed | tf_op | source)
XLA Modules:
  0.0 920.8 jit_solution(12152243749214164985)
XLA Ops:
  12.3 50.2 %all-gather.4.cloned.1.call-done = f32[64,8192]{1,0:T(8,128)} async-done(((f32[64,1024]{1,0:T(8,128)}), f32[64,8192]{1,0:T(8,128)}) %all-gather.4.cloned.1.call-update) | async-done | bytes 2097168 | tf_op jit(solution)/shard_map/all_gather | solution.py:53
  64.4 7.0 gather_fusion
  71.4 37.3 %broadcast_multiply_fusion.3 = f32[512,64,128]{2,1,0:T(8,128)} fusion(f32[512]{0:T(512)S(1)} %get-tuple-element.8, bf16[1,1,512,128,128]{4,3,2,1,0:T(8,128)(2,1)} %param.17, f32[512,64,128]{2,1,0:T(8,128)} %gather_fusion, pred[512]{0:T(512)(128)(4,1)S(1)} %get-tuple-element.9), kind=kOutput, calls=%fused_computation.32 | convolution fusion | flops 6450839552 | bytes 50334208 | tf_op jit(solution)/shard_map/ktc,trc->ktr/dot_general | solution.py:26
  108.9 51.8 %scatter_fusion = f32[64,64,128]{2,0,1:T(8,128)S(1)} fusion(f32[64,64,128]{2,0,1:T(8,128)S(1)} %broadcast.101.clone.2, s32[512]{0:T(512)S(1)} %bitcast.126, f32[512,64,128]{2,1,0:T(8,128)} %broadcast_multiply_fusion.3), kind=kCustom, calls=%fused_computation.4 | custom fusion | flops 4194304 | bytes 50333696 | tf_op jit(solution)/shard_map/scatter-add | solution.py:34
  163.0 29.2 %reduce-scatter.3.cloned.1.call-done = f32[64,2048]{1,0:T(8,128)} async-done(((f32[64,8192]{1,0:T(8,128)}), f32[64,2048]{1,0:T(8,128)}) %reduce-scatter.3.cloned.1.call-update) | async-done | bytes 524304 | tf_op jit(solution)/shard_map/reduce_scatter | solution.py:79
  194.0 39.4 %psum.42 = f32[64,64]{0,1:T(8,128)S(1)} all-reduce(f32[64,64]{0,1:T(8,128)S(1)} %fusion.59), channel_id=1, replica_groups=mesh['users'=8,'items'=4] {'users','items'}, use_global_device_ids=true, to_apply=%region_2.4 | all-reduce | flops 4096 | bytes 32768 | tf_op jit(solution)/shard_map/psum | solution.py:82
  248.8 22.8 %all-gather.6.cloned.1.call-done = f32[64,8192]{1,0:T(8,128)} async-done(((f32[64,2048]{1,0:T(8,128)}), f32[64,8192]{1,0:T(8,128)}) %all-gather.6.cloned.1.call-update) | async-done | bytes 2097168 | tf_op jit(solution)/shard_map/all_gather | solution.py:84
  273.4 7.0 gather_fusion.1
  280.4 22.0 %broadcast_multiply_fusion.2 = f32[512,64,128]{2,1,0:T(8,128)} fusion(f32[512]{0:T(512)S(1)} %get-tuple-element.8, bf16[1,1,512,128,128]{4,3,2,1,0:T(8,128)(2,1)} %param.17, f32[512,64,128]{2,1,0:T(8,128)} %gather_fusion.1, pred[512]{0:T(512)(128)(4,1)S(1)} %compare_and_fusion.1), kind=kOutput, calls=%fused_computation.31 | convolution fusion | flops 6450839552 | bytes 50334208 | tf_op jit(solution)/shard_map/ktr,trc->ktc/dot_general | solution.py:40
  302.7 51.9 %scatter_fusion.1 = f32[64,64,128]{2,0,1:T(8,128)S(1)} fusion(f32[64,64,128]{2,0,1:T(8,128)S(1)} %broadcast.101.clone.1, s32[512]{0:T(512)S(1)} %bitcast.128, f32[512,64,128]{2,1,0:T(8,128)} %broadcast_multiply_fusion.2), kind=kCustom, calls=%fused_computation.5 | custom fusion | flops 4194304 | bytes 50333696 | tf_op jit(solution)/shard_map/scatter-add | solution.py:48
  356.1 31.5 %all_gather.12 = f32[8192]{0:T(1024)S(1)} all-gather(f32[1024]{0:T(1024)S(1)} %convert_rsqrt_fusion.1), channel_id=1, replica_groups=mesh['users'=8,'items'=4] {'users'}, dimensions={0}, use_global_device_ids=true | all-gather | bytes 36864 | tf_op jit(solution)/shard_map/all_gather | solution.py:70
  387.6 71.1 %all-reduce.3.cloned.1.call-done = f32[64,8192]{1,0:T(8,128)} async-done(((f32[64,8192]{1,0:T(8,128)}), f32[64,8192]{1,0:T(8,128)}) %all-reduce.3.cloned.1.call-update) | async-done | bytes 2097168 | tf_op jit(solution)/shard_map/psum | solution.py:86
  463.0 10.9 %psum.44 = f32[64,64]{0,1:T(8,128)S(1)} all-reduce(f32[64,64]{0,1:T(8,128)S(1)} %fusion.45), channel_id=1, replica_groups=mesh['users'=8,'items'=4] {'items'}, use_global_device_ids=true, to_apply=%region_7.0 | all-reduce | flops 4096 | bytes 32768 | tf_op jit(solution)/shard_map/psum | solution.py:87
  488.4 7.0 gather_fusion.2
  495.4 37.3 %broadcast_multiply_fusion.1 = f32[512,64,128]{2,1,0:T(8,128)} fusion(f32[512]{0:T(512)S(1)} %get-tuple-element.8, bf16[1,1,512,128,128]{4,3,2,1,0:T(8,128)(2,1)} %param.17, f32[512,64,128]{2,1,0:T(8,128)} %gather_fusion.2, pred[512]{0:T(512)(128)(4,1)S(1)} %get-tuple-element.9), kind=kOutput, calls=%fused_computation.30 | convolution fusion | flops 6450839552 | bytes 50334208 | tf_op jit(solution)/shard_map/ktc,trc->ktr/dot_general | solution.py:26
  532.9 51.8 %scatter_fusion.2 = f32[64,64,128]{2,0,1:T(8,128)S(1)} fusion(f32[64,64,128]{2,0,1:T(8,128)S(1)} %broadcast.101.clone, s32[512]{0:T(512)S(1)} %bitcast.127, f32[512,64,128]{2,1,0:T(8,128)} %broadcast_multiply_fusion.1), kind=kCustom, calls=%fused_computation.6 | custom fusion | flops 4194304 | bytes 50333696 | tf_op jit(solution)/shard_map/scatter-add | solution.py:34
  586.6 30.1 %reduce-scatter.5.cloned.1.call-done = f32[64,2048]{1,0:T(8,128)} async-done(((f32[64,8192]{1,0:T(8,128)}), f32[64,2048]{1,0:T(8,128)}) %reduce-scatter.5.cloned.1.call-update) | async-done | bytes 524304 | tf_op jit(solution)/shard_map/reduce_scatter | solution.py:79
  618.5 39.4 %psum.45 = f32[64,64]{0,1:T(8,128)S(1)} all-reduce(f32[64,64]{0,1:T(8,128)S(1)} %fusion.56), channel_id=1, replica_groups=mesh['users'=8,'items'=4] {'users','items'}, use_global_device_ids=true, to_apply=%region_10.15 | all-reduce | flops 4096 | bytes 32768 | tf_op jit(solution)/shard_map/psum | solution.py:82
  672.9 23.4 %all-gather.8.cloned.1.call-done = f32[64,8192]{1,0:T(8,128)} async-done(((f32[64,2048]{1,0:T(8,128)}), f32[64,8192]{1,0:T(8,128)}) %all-gather.8.cloned.1.call-update) | async-done | bytes 2097168 | tf_op jit(solution)/shard_map/all_gather | solution.py:84
  698.2 7.0 gather_fusion.3
  705.2 22.0 %broadcast_multiply_fusion = f32[512,64,128]{2,1,0:T(8,128)} fusion(f32[512]{0:T(512)S(1)} %get-tuple-element.8, bf16[1,1,512,128,128]{4,3,2,1,0:T(8,128)(2,1)} %param.17, f32[512,64,128]{2,1,0:T(8,128)} %gather_fusion.3, pred[512]{0:T(512)(128)(4,1)S(1)} %compare_and_fusion.1), kind=kOutput, calls=%fused_computation.29 | convolution fusion | flops 6450839552 | bytes 50334208 | tf_op jit(solution)/shard_map/ktr,trc->ktc/dot_general | solution.py:40
  727.4 51.9 %scatter_fusion.3 = f32[64,64,128]{2,0,1:T(8,128)S(1)} fusion(f32[64,64,128]{2,0,1:T(8,128)S(1)} %broadcast.101, s32[512]{0:T(512)S(1)} %bitcast.129, f32[512,64,128]{2,1,0:T(8,128)} %broadcast_multiply_fusion), kind=kCustom, calls=%fused_computation.7 | custom fusion | flops 4194304 | bytes 50333696 | tf_op jit(solution)/shard_map/scatter-add | solution.py:48
  780.8 102.5 %all-reduce.5.cloned.1.call-done = f32[64,8192]{1,0:T(8,128)} async-done(((f32[64,8192]{1,0:T(8,128)}), f32[64,8192]{1,0:T(8,128)}) %all-reduce.5.cloned.1.call-update) | async-done | bytes 2097168 | tf_op jit(solution)/shard_map/psum | solution.py:86
  887.6 11.0 %psum.47 = f32[64,64]{0,1:T(8,128)S(1)} all-reduce(f32[64,64]{0,1:T(8,128)S(1)} %fusion.42), channel_id=1, replica_groups=mesh['users'=8,'items'=4] {'items'}, use_global_device_ids=true, to_apply=%region_13.18 | all-reduce | flops 4096 | bytes 32768 | tf_op jit(solution)/shard_map/psum | solution.py:87
  (88 shorter events, 89.6 us)
Async XLA Ops:
  7.2 55.4 %all-gather.4.cloned.1.call-start = ((), (), s32[]{:S(2)}) async-start(), calls=%async_computation.2 | async-start | bytes 2359296 | tf_op jit(solution)/shard_map/all_gather | solution.py:53
  9.6 182.6 %reduce-scatter.3.cloned.1.call-start = ((), (), s32[]{:S(2)}) async-start(), calls=%async_computation.3 | async-start | bytes 2621440 | tf_op jit(solution)/shard_map/reduce_scatter | solution.py:79
  162.3 0.7 copy-start.4
  162.3 86.4 %copy-start.2 = (s32[1,1,512]{2,1,0:T(1,128)S(1)}, s32[1,1,512]{2,1,0:T(1,128)}, u32[]{:S(2)}) copy-start(s32[1,1,512]{2,1,0:T(1,128)} %param.14) | copy-start | bytes 6148
  162.3 86.5 %copy-start.3 = (s32[1,1,512]{2,1,0:T(1,128)S(1)}, s32[1,1,512]{2,1,0:T(1,128)}, u32[]{:S(2)}) copy-start(s32[1,1,512]{2,1,0:T(1,128)} %param.15) | copy-start | bytes 6148
  162.3 109.3 %all-gather.6.cloned.1.call-start = ((), (), s32[]{:S(2)}) async-start(), calls=%async_computation.4 | async-start | bytes 2621440 | tf_op jit(solution)/shard_map/all_gather | solution.py:84
  248.1 210.5 %all-reduce.3.cloned.1.call-start = ((), (), s32[]{:S(2)}) async-start(), calls=%async_computation.5 | async-start | bytes 4194304 | tf_op jit(solution)/shard_map/psum | solution.py:86
  356.0 260.7 %reduce-scatter.5.cloned.1.call-start = ((), (), s32[]{:S(2)}) async-start(), calls=%async_computation.6 | async-start | bytes 2621440 | tf_op jit(solution)/shard_map/reduce_scatter | solution.py:79
  458.7 27.4 %copy-start.1 = (f32[64,8192]{1,0:T(8,128)S(1)}, f32[64,8192]{1,0:T(8,128)}, u32[]{:S(2)}) copy-start(f32[64,8192]{1,0:T(8,128)} %all-reduce.3.cloned.1.call-done) | copy-start | bytes 6291460
  586.3 110.0 %all-gather.8.cloned.1.call-start = ((), (), s32[]{:S(2)}) async-start(), calls=%async_computation.7 | async-start | bytes 2621440 | tf_op jit(solution)/shard_map/all_gather | solution.py:84
  672.8 210.4 %all-reduce.5.cloned.1.call-start = ((), (), s32[]{:S(2)}) async-start(), calls=%async_computation.8 | async-start | bytes 4194304 | tf_op jit(solution)/shard_map/psum | solution.py:86
  883.2 27.5 %copy-start = (f32[64,8192]{1,0:T(8,128)S(1)}, f32[64,8192]{1,0:T(8,128)}, u32[]{:S(2)}) copy-start(f32[64,8192]{1,0:T(8,128)} %all-reduce.5.cloned.1.call-done) | copy-start | bytes 6291460
Sparse Core Ops, SparseCore 0:
  10.7 51.7 all-gather.3
  162.4 29.7 reduce-scatter.2
  248.3 23.2 all-gather.5
  356.1 102.5 all-reduce.2
  586.4 30.2 reduce-scatter.4
  673.0 23.3 all-gather.7
  780.9 102.3 all-reduce.4
where the time goes:
time: 936 us; the launch traced here: 921 us
  waiting for transfers between devices  329 us (35%)
  other arithmetic  260 us (28%)
  matrix products  140 us (15%)
  blocking collectives  132 us (14%)
  local copies, waits for them, and re-layouts  42.2 us (5%)
  between operations  15.6 us (2%)
    psum x2, waiting for transfers between devices, body(): item_raw = item_scale_block[None, :] * lax.psum(partial_items, 'users')  174 us
    scatter-add x2, other arithmetic, item_partial(): summed = jnp.zeros((K, IT, TILE), jnp.float32).at[:, cols, :].add(product)  104 us
    scatter-add x2, other arithmetic, user_partial(): summed = jnp.zeros((K, UT, TILE), jnp.float32).at[:, rows, :].add(product)  104 us
    psum x2, blocking collectives, body(): user_gram = lax.psum(local_gram(user_raw), ('users', 'items'))  78.9 us
    dot_general x2, matrix products, user_partial(): jnp.einsum('ktc,trc->ktr', picked, values, precision=lax.Precision.HIGHES...  74.6 us
    reduce_scatter x2, waiting for transfers between devices, body(): lax.psum_scatter(partial_users, 'items', scatter_dimension=1, tiled=True)  59.4 us
    all_gather x1, waiting for transfers between devices, gather_items(): return lax.all_gather(sent, 'users', axis=1, tiled=True)  50.2 us
    all_gather x2, waiting for transfers between devices, body(): lax.all_gather(user_scale[None, :] * user_panel, 'items', axis=1, tiled=T...  46.2 us
  transfers between devices with their start and end apart: 7, of which 7 were waited for; matrix products, arithmetic and copies ran while one was open for 0% of the time, Pallas kernels for 0%

commit v1 on v0

--- a/solution.py
+++ b/solution.py
@@ -83,7 +83,9 @@
         user_panel = solve_panel(user_gram / user_total, user_raw)
         full_users = lax.all_gather(user_scale[None, :] * user_panel, "items", axis=1, tiled=True)
         partial_items = item_partial(full_users, rows, cols, values, live_weight)
-        item_raw = item_scale_block[None, :] * lax.psum(partial_items, "users")
+        item_raw = item_scale_block[None, :] * jnp.sum(
+            lax.all_gather(partial_items, "users"), axis=0
+        )
         item_gram = lax.psum(local_gram(item_raw), "items")
         panel = solve_panel(item_gram / item_total, item_raw)
     item_out = lax.dynamic_slice_in_dim(panel, lax.axis_index("users") * item_width, item_width, 1)

time: 936 us -> 1200 us (1.28)
  waiting for transfers between devices: 329 us -> 579 us
  other arithmetic: 260 us -> 274 us
    all_gather x0 -> x2, waiting for transfers between devices: none -> 423 us  [body(): lax.all_gather(partial_items, 'users')]
    psum x2 -> x0, waiting for transfers between devices: 174 us -> none  [body(): item_raw = item_scale_block[None, :] * lax.psum(partial_items, 'users')]
    reduce_sum x0 -> x2, other arithmetic: none -> 13.9 us  [body(): jnp.sum(lax.all_gather(partial_items, 'users'), axis=0)]
where the time goes in v1:
time: 1200 us; the launch traced here: 1190 us
  waiting for transfers between devices  579 us (48%)
  other arithmetic  274 us (23%)
  matrix products  135 us (11%)
  blocking collectives  132 us (11%)
  local copies, waits for them, and re-layouts  49.4 us (4%)
  between operations  15.4 us (1%)
    all_gather x2, waiting for transfers between devices, body(): lax.all_gather(partial_items, 'users')  423 us
    scatter-add x2, other arithmetic, item_partial(): summed = jnp.zeros((K, IT, TILE), jnp.float32).at[:, cols, :].add(product)  104 us
    scatter-add x2, other arithmetic, user_partial(): summed = jnp.zeros((K, UT, TILE), jnp.float32).at[:, rows, :].add(product)  104 us
    psum x2, blocking collectives, body(): user_gram = lax.psum(local_gram(user_raw), ('users', 'items'))  78.9 us
    dot_general x2, matrix products, user_partial(): jnp.einsum('ktc,trc->ktr', picked, values, precision=lax.Precision.HIGHES...  74.6 us
    reduce_scatter x2, waiting for transfers between devices, body(): lax.psum_scatter(partial_users, 'items', scatter_dimension=1, tiled=True)  58.9 us
    all_gather x1, waiting for transfers between devices, gather_items(): return lax.all_gather(sent, 'users', axis=1, tiled=True)  50.2 us
    all_gather x2, waiting for transfers between devices, body(): lax.all_gather(user_scale[None, :] * user_panel, 'items', axis=1, tiled=T...  46.5 us
  transfers between devices with their start and end apart: 7, of which 7 were waited for; matrix products, arithmetic and copies ran while one was open for 0% of the time, Pallas kernels for 0%

profile of v1, /device:TPU:0, one launch (start us, length us, event | category | flops | bytes accessed | tf_op | source)
XLA Modules:
  0.0 1185.6 jit_solution(12848220462504709427)
XLA Ops:
  12.3 50.2 %all-gather.6.cloned.1.call-done = f32[64,8192]{1,0:T(8,128)} async-done(((f32[64,1024]{1,0:T(8,128)}), f32[64,8192]{1,0:T(8,128)}) %all-gather.6.cloned.1.call-update) | async-done | bytes 2097168 | tf_op jit(solution)/shard_map/all_gather | solution.py:53
  64.4 7.0 gather_fusion
  71.4 37.3 %broadcast_multiply_fusion.3 = f32[512,64,128]{2,1,0:T(8,128)} fusion(f32[512]{0:T(512)S(1)} %get-tuple-element.8, bf16[1,1,512,128,128]{4,3,2,1,0:T(8,128)(2,1)} %param.17, f32[512,64,128]{2,1,0:T(8,128)} %gather_fusion, pred[512]{0:T(512)(128)(4,1)S(1)} %get-tuple-element.9), kind=kOutput, calls=%fused_computation.32 | convolution fusion | flops 6450839552 | bytes 50334208 | tf_op jit(solution)/shard_map/ktc,trc->ktr/dot_general | solution.py:26
  108.9 51.8 %scatter_fusion = f32[64,64,128]{2,0,1:T(8,128)S(1)} fusion(f32[64,64,128]{2,0,1:T(8,128)S(1)} %broadcast.101.clone.2, s32[512]{0:T(512)S(1)} %bitcast.116, f32[512,64,128]{2,1,0:T(8,128)} %broadcast_multiply_fusion.3), kind=kCustom, calls=%fused_computation.4 | custom fusion | flops 4194304 | bytes 50333696 | tf_op jit(solution)/shard_map/scatter-add | solution.py:34
  162.4 29.8 %reduce-scatter.3.cloned.1.call-done = f32[64,2048]{1,0:T(8,128)} async-done(((f32[64,8192]{1,0:T(8,128)}), f32[64,2048]{1,0:T(8,128)}) %reduce-scatter.3.cloned.1.call-update) | async-done | bytes 524304 | tf_op jit(solution)/shard_map/reduce_scatter | solution.py:79
  194.0 39.4 %psum.28 = f32[64,64]{0,1:T(8,128)S(1)} all-reduce(f32[64,64]{0,1:T(8,128)S(1)} %fusion.59), channel_id=1, replica_groups=mesh['users'=8,'items'=4] {'users','items'}, use_global_device_ids=true, to_apply=%region_2.4 | all-reduce | flops 4096 | bytes 32768 | tf_op jit(solution)/shard_map/psum | solution.py:82
  248.5 23.2 %all-gather.8.cloned.1.call-done = f32[64,8192]{1,0:T(8,128)} async-done(((f32[64,2048]{1,0:T(8,128)}), f32[64,8192]{1,0:T(8,128)}) %all-gather.8.cloned.1.call-update) | async-done | bytes 2097168 | tf_op jit(solution)/shard_map/all_gather | solution.py:84
  273.5 7.0 gather_fusion.1
  280.5 22.0 %broadcast_multiply_fusion.2 = f32[512,64,128]{2,1,0:T(8,128)} fusion(f32[512]{0:T(512)S(1)} %get-tuple-element.8, bf16[1,1,512,128,128]{4,3,2,1,0:T(8,128)(2,1)} %param.17, f32[512,64,128]{2,1,0:T(8,128)} %gather_fusion.1, pred[512]{0:T(512)(128)(4,1)S(1)} %compare_and_fusion.1), kind=kOutput, calls=%fused_computation.31 | convolution fusion | flops 6450839552 | bytes 50334208 | tf_op jit(solution)/shard_map/ktr,trc->ktc/dot_general | solution.py:40
  302.7 51.9 %scatter_fusion.1 = f32[64,64,128]{2,0,1:T(8,128)S(1)} fusion(f32[64,64,128]{2,0,1:T(8,128)S(1)} %broadcast.101.clone.1, s32[512]{0:T(512)S(1)} %bitcast.118, f32[512,64,128]{2,1,0:T(8,128)} %broadcast_multiply_fusion.2), kind=kCustom, calls=%fused_computation.5 | custom fusion | flops 4194304 | bytes 50333696 | tf_op jit(solution)/shard_map/scatter-add | solution.py:48
  360.0 31.5 %all_gather.18 = f32[8192]{0:T(1024)S(1)} all-gather(f32[1024]{0:T(1024)S(1)} %convert_rsqrt_fusion.1), channel_id=1, replica_groups=mesh['users'=8,'items'=4] {'users'}, dimensions={0}, use_global_device_ids=true | all-gather | bytes 36864 | tf_op jit(solution)/shard_map/all_gather | solution.py:70
  391.5 196.0 %all-gather.10.cloned.1.call-done = f32[8,64,8192]{2,1,0:T(8,128)} async-done(((f32[1,64,8192]{2,1,0:T(8,128)}), f32[8,64,8192]{2,1,0:T(8,128)}) %all-gather.10.cloned.1.call-update) | async-done | bytes 16777232 | tf_op jit(solution)/shard_map/all_gather | solution.py:87
  596.3 10.6 psum.29
  621.5 7.0 gather_fusion.2
  628.4 37.3 %broadcast_multiply_fusion.1 = f32[512,64,128]{2,1,0:T(8,128)} fusion(f32[512]{0:T(512)S(1)} %get-tuple-element.8, bf16[1,1,512,128,128]{4,3,2,1,0:T(8,128)(2,1)} %param.17, f32[512,64,128]{2,1,0:T(8,128)} %gather_fusion.2, pred[512]{0:T(512)(128)(4,1)S(1)} %get-tuple-element.9), kind=kOutput, calls=%fused_computation.30 | convolution fusion | flops 6450839552 | bytes 50334208 | tf_op jit(solution)/shard_map/ktc,trc->ktr/dot_general | solution.py:26
  666.0 51.8 %scatter_fusion.2 = f32[64,64,128]{2,0,1:T(8,128)S(1)} fusion(f32[64,64,128]{2,0,1:T(8,128)S(1)} %broadcast.101.clone, s32[512]{0:T(512)S(1)} %bitcast.117, f32[512,64,128]{2,1,0:T(8,128)} %broadcast_multiply_fusion.1), kind=kCustom, calls=%fused_computation.6 | custom fusion | flops 4194304 | bytes 50333696 | tf_op jit(solution)/shard_map/scatter-add | solution.py:34
  719.8 29.1 %reduce-scatter.5.cloned.1.call-done = f32[64,2048]{1,0:T(8,128)} async-done(((f32[64,8192]{1,0:T(8,128)}), f32[64,2048]{1,0:T(8,128)}) %reduce-scatter.5.cloned.1.call-update) | async-done | bytes 524304 | tf_op jit(solution)/shard_map/reduce_scatter | solution.py:79
  750.7 39.5 %psum.30 = f32[64,64]{0,1:T(8,128)S(1)} all-reduce(f32[64,64]{0,1:T(8,128)S(1)} %fusion.56), channel_id=1, replica_groups=mesh['users'=8,'items'=4] {'users','items'}, use_global_device_ids=true, to_apply=%region_10.15 | all-reduce | flops 4096 | bytes 32768 | tf_op jit(solution)/shard_map/psum | solution.py:82
  805.1 23.4 %all-gather.12.cloned.1.call-done = f32[64,8192]{1,0:T(8,128)} async-done(((f32[64,2048]{1,0:T(8,128)}), f32[64,8192]{1,0:T(8,128)}) %all-gather.12.cloned.1.call-update) | async-done | bytes 2097168 | tf_op jit(solution)/shard_map/all_gather | solution.py:84
  830.4 7.0 gather_fusion.3
  837.4 22.0 %broadcast_multiply_fusion = f32[512,64,128]{2,1,0:T(8,128)} fusion(f32[512]{0:T(512)S(1)} %get-tuple-element.8, bf16[1,1,512,128,128]{4,3,2,1,0:T(8,128)(2,1)} %param.17, f32[512,64,128]{2,1,0:T(8,128)} %gather_fusion.3, pred[512]{0:T(512)(128)(4,1)S(1)} %compare_and_fusion.1), kind=kOutput, calls=%fused_computation.29 | convolution fusion | flops 6450839552 | bytes 50334208 | tf_op jit(solution)/shard_map/ktr,trc->ktc/dot_general | solution.py:40
  859.7 51.9 %scatter_fusion.3 = f32[64,64,128]{2,0,1:T(8,128)S(1)} fusion(f32[64,64,128]{2,0,1:T(8,128)S(1)} %broadcast.101, s32[512]{0:T(512)S(1)} %bitcast.119, f32[512,64,128]{2,1,0:T(8,128)} %broadcast_multiply_fusion), kind=kCustom, calls=%fused_computation.7 | custom fusion | flops 4194304 | bytes 50333696 | tf_op jit(solution)/shard_map/scatter-add | solution.py:48
  916.9 227.4 %all-gather.14.cloned.1.call-done = f32[8,64,8192]{2,1,0:T(8,128)} async-done(((f32[1,64,8192]{2,1,0:T(8,128)}), f32[8,64,8192]{2,1,0:T(8,128)}) %all-gather.14.cloned.1.call-update) | async-done | bytes 16777232 | tf_op jit(solution)/shard_map/all_gather | solution.py:87
  1153.1 10.6 psum.31
  (88 shorter events, 105.5 us)
Async XLA Ops:
  7.2 55.4 %all-gather.6.cloned.1.call-start = ((), (), s32[]{:S(2)}) async-start(), calls=%async_computation.2 | async-start | bytes 2359296 | tf_op jit(solution)/shard_map/all_gather | solution.py:53
  9.6 182.7 %reduce-scatter.3.cloned.1.call-start = ((), (), s32[]{:S(2)}) async-start(), calls=%async_computation.3 | async-start | bytes 2621440 | tf_op jit(solution)/shard_map/reduce_scatter | solution.py:79
  160.8 1.6 copy-start.2
  160.8 87.6 %copy-start = (s32[1,1,512]{2,1,0:T(1,128)S(1)}, s32[1,1,512]{2,1,0:T(1,128)}, u32[]{:S(2)}) copy-start(s32[1,1,512]{2,1,0:T(1,128)} %param.14) | copy-start | bytes 6148
  160.8 87.6 %copy-start.1 = (s32[1,1,512]{2,1,0:T(1,128)S(1)}, s32[1,1,512]{2,1,0:T(1,128)}, u32[]{:S(2)}) copy-start(s32[1,1,512]{2,1,0:T(1,128)} %param.15) | copy-start | bytes 6148
  162.3 109.3 %all-gather.8.cloned.1.call-start = ((), (), s32[]{:S(2)}) async-start(), calls=%async_computation.4 | async-start | bytes 2621440 | tf_op jit(solution)/shard_map/all_gather | solution.py:84
  248.2 339.4 %all-gather.10.cloned.1.call-start = ((), (), s32[]{:S(2)}) async-start(), calls=%async_computation.5 | async-start | bytes 18874368 | tf_op jit(solution)/shard_map/all_gather | solution.py:87
  360.0 389.0 %reduce-scatter.5.cloned.1.call-start = ((), (), s32[]{:S(2)}) async-start(), calls=%async_computation.6 | async-start | bytes 2621440 | tf_op jit(solution)/shard_map/reduce_scatter | solution.py:79
  719.3 109.2 %all-gather.12.cloned.1.call-start = ((), (), s32[]{:S(2)}) async-start(), calls=%async_computation.7 | async-start | bytes 2621440 | tf_op jit(solution)/shard_map/all_gather | solution.py:84
  805.1 339.2 %all-gather.14.cloned.1.call-start = ((), (), s32[]{:S(2)}) async-start(), calls=%async_computation.8 | async-start | bytes 18874368 | tf_op jit(solution)/shard_map/all_gather | solution.py:87
Sparse Core Ops, SparseCore 0:
  10.7 51.7 all-gather.5
  162.5 29.7 reduce-scatter.2
  248.3 23.2 all-gather.7
  360.1 227.4 all-gather.9
  719.5 29.4 reduce-scatter.4
  805.2 23.2 all-gather.11
  917.0 227.2 all-gather.13
